TPU v7x, 32 devices: a whole 2x2x4 slice. The times are simulated.
32 devices in a mesh: batch: 2 (over y), seq: 16 (over z, x, core).
Axes of the slice: x: 2, y: 2, z: 4, core: 2. Of those that a mesh axis runs over, the one named last changes fastest.
Arguments:
- inputs: bfloat16 [2, 2, 1024, 768], P(None, 'batch', 'seq'), may hold values from -6 to 6
- params: bfloat16 [7087104], P(('batch', 'seq')), may hold values from -3 to 3, as said below
- segment_ids: int32 [2, 2, 1024], P(None, 'batch'), may hold values from 0 to 15, never falling along the last dimension, each value on 1 to 512 neighbouring positions
- cotangent: bfloat16 [2, 2, 1024, 768], P(None, 'batch', 'seq'), may hold values from -6 to 6
Outputs:
- outputs: bfloat16 [2, 2, 1024, 768], P(None, 'batch', 'seq')
- input_grad: bfloat16 [2, 2, 1024, 768], P(None, 'batch', 'seq')
- param_grad: float32 [7087104], P(('batch', 'seq'))
Inputs may be any that keep to these rules, and one draw needn't show every extreme that they name: params holds one after another, each matrix row by row and applied as x times the matrix: w_query, w_key, w_value, w_out (768 x 768 each), w_in (768 x 3072), w_down (3072 x 768), b_query, b_value, b_out, gain_one, shift_one (768 each), b_in (3072), b_down, gain_two, shift_two (768 each). `segment_ids`: ids never fall along a sequence; a document has 1 to 512 tokens.
All inputs are finite; a program needn't handle non-finite values.
Results may differ from a plain program's by a relative error of at most 0.013.
Values may be sent and summed in bfloat16 or wider, within the bound.
No kernel may reach another device: no remote copies, remote signals or barrier semaphores. Data moves between devices by JAX's collectives and lax.ppermute only.
A program may use at most 320 MiB of HBM per device.

v0:
```python
from functools import partial
import math

import jax
import jax.numpy as jnp
from jax import lax
from jax.sharding import PartitionSpec as P

D = 768
HD = 64
FF = 3072


epsilon = 1e-12


def unpack_params(flat_params):
    layout = [
        (D, D),
        (D, D),
        (D, D),
        (D, D),
        (D, FF),
        (FF, D),
        (D,),
        (D,),
        (D,),
        (D,),
        (D,),
        (FF,),
        (D,),
        (D,),
        (D,),
    ]
    pieces_list = []
    offset = 0
    for extent in layout:
        entry_count = math.prod(extent)
        pieces_list.append(flat_params[offset : offset + entry_count].reshape(extent))
        offset += entry_count
    return pieces_list


def layer_norm(values_in, gain_vec, shift_vec):
    average = jnp.mean(values_in, axis=-1, keepdims=True)
    centred = values_in - average
    variance = jnp.mean(centred * centred, axis=-1, keepdims=True)
    return centred * lax.rsqrt(variance + epsilon) * gain_vec + shift_vec


def project(left_side, right_side):
    return jnp.dot(left_side, right_side, preferred_element_type=jnp.float32)


def outer_product(left_side, right_side):
    return lax.dot_general(
        left_side, right_side, (((0,), (0,)), ((), ())), preferred_element_type=jnp.float32
    )


def backward_product(left_side, right_side):
    return lax.dot_general(
        left_side, right_side, (((1,), (1,)), ((), ())), preferred_element_type=jnp.float32
    )


def column_sum(matrix):
    return jnp.sum(matrix.astype(jnp.float32), axis=0)


def masked_scores(query_group, key_group, same_doc, scale):
    scores = (
        jnp.einsum("qhd,khd->hqk", query_group, key_group, preferred_element_type=jnp.float32)
        * scale
    )
    return jnp.where(same_doc[None], scores, -1e30)


def soft_weights(query_group, key_group, same_doc, scale):
    return jax.nn.softmax(masked_scores(query_group, key_group, same_doc, scale), axis=-1)


def body(inputs, params, segment_ids, cotangent):
    row_count = inputs.shape[2]
    micro_count = inputs.shape[0]
    position = lax.axis_index("seq") * row_count
    scale = HD ** (-0.5)
    head_group = 4
    group_width = head_group * HD
    grad_total = None
    output_list = []
    input_grad_list = []
    for micro_step in range(micro_count):
        gathered = lax.all_gather(params, ("batch", "seq"), axis=0, tiled=True)
        (
            w_query,
            w_key,
            w_value,
            w_out,
            w_in,
            w_down,
            b_query,
            b_value,
            b_out,
            gain_one,
            shift_one,
            b_in,
            b_down,
            gain_two,
            shift_two,
        ) = unpack_params(gathered)
        tokens = inputs[micro_step, 0]
        segment_row = segment_ids[micro_step, 0]
        segment_own = lax.dynamic_slice_in_dim(segment_row, position, row_count)
        same_doc = segment_own[:, None] == segment_row[None, :]
        query = (project(tokens, w_query) + b_query).astype(jnp.bfloat16)
        keys_own = project(tokens, w_key).astype(jnp.bfloat16)
        values_own = (project(tokens, w_value) + b_value).astype(jnp.bfloat16)
        keys_all, values_all = (
            lax.all_gather(keys_own, "seq", axis=0, tiled=True),
            lax.all_gather(values_own, "seq", axis=0, tiled=True),
        )
        length_all = keys_all.shape[0]

        def head_slices(column):
            return (
                query[:, column : column + group_width].reshape(row_count, head_group, HD),
                keys_all[:, column : column + group_width].reshape(length_all, head_group, HD),
                values_all[:, column : column + group_width].reshape(length_all, head_group, HD),
            )

        attended_list = []
        for column in range(0, D, group_width):
            query_group, key_group, value_group = head_slices(column)
            probability = soft_weights(query_group, key_group, same_doc, scale).astype(jnp.bfloat16)
            attended_list.append(
                jnp.einsum(
                    "hqk,khd->qhd", probability, value_group, preferred_element_type=jnp.float32
                ).reshape(row_count, group_width)
            )
        attended = jnp.concatenate(attended_list, axis=1).astype(jnp.bfloat16)
        branch = project(attended, w_out) + b_out
        residual_one = tokens.astype(jnp.float32) + branch
        gain_one_f, shift_one_f = (gain_one.astype(jnp.float32), shift_one.astype(jnp.float32))
        gain_two_f, shift_two_f = (gain_two.astype(jnp.float32), shift_two.astype(jnp.float32))
        first_norm = layer_norm(residual_one, gain_one_f, shift_one_f)
        first_low = first_norm.astype(jnp.bfloat16)
        inner_act = project(first_low, w_in) + b_in
        gelu_exact = partial(jax.nn.gelu, approximate=False)
        hidden_low = gelu_exact(inner_act).astype(jnp.bfloat16)
        second = project(hidden_low, w_down) + b_down
        residual_two = first_norm + second
        output_list.append(layer_norm(residual_two, gain_two_f, shift_two_f).astype(jnp.bfloat16))
        gathered = lax.all_gather(params, ("batch", "seq"), axis=0, tiled=True)
        (
            w_query,
            w_key,
            w_value,
            w_out,
            w_in,
            w_down,
            b_query,
            b_value,
            b_out,
            gain_one,
            shift_one,
            b_in,
            b_down,
            gain_two,
            shift_two,
        ) = unpack_params(gathered)
        grad_out = cotangent[micro_step, 0].astype(jnp.float32)
        norm_two_out, pull_two = jax.vjp(layer_norm, residual_two, gain_two_f, shift_two_f)
        d_res_two, d_gain_two, d_shift_two = pull_two(grad_out)
        d_second = d_res_two.astype(jnp.bfloat16)
        d_w_down = outer_product(hidden_low, d_second)
        d_b_down = column_sum(d_second)
        d_hidden = backward_product(d_second, w_down)
        gelu_out, pull_gelu = jax.vjp(gelu_exact, inner_act)
        d_inner = pull_gelu(d_hidden)[0].astype(jnp.bfloat16)
        d_w_in = outer_product(first_low, d_inner)
        d_b_in = column_sum(d_inner)
        d_first = d_res_two + backward_product(d_inner, w_in)
        norm_one_out, pull_one = jax.vjp(layer_norm, residual_one, gain_one_f, shift_one_f)
        d_res_one, d_gain_one, d_shift_one = pull_one(d_first)
        d_branch = d_res_one.astype(jnp.bfloat16)
        d_w_out = outer_product(attended, d_branch)
        d_b_out = column_sum(d_branch)
        d_attended = backward_product(d_branch, w_out).astype(jnp.bfloat16)
        query_grad_list = []
        key_grad_list = []
        value_grad_list = []
        log_sum_list = []
        delta_list = []
        for column in range(0, D, group_width):
            query_group, key_group, value_group = head_slices(column)
            masked = masked_scores(query_group, key_group, same_doc, scale)
            log_sum = jax.nn.logsumexp(masked, axis=-1)
            probability = jnp.exp(masked - log_sum[:, :, None])
            probability_low = probability.astype(jnp.bfloat16)
            d_group = d_attended[:, column : column + group_width].reshape(
                row_count, head_group, HD
            )
            d_prob = jnp.einsum(
                "qhd,khd->hqk", d_group, value_group, preferred_element_type=jnp.float32
            )
            delta_row = jnp.sum(probability * d_prob, axis=-1)
            d_scores = (probability * (d_prob - delta_row[:, :, None])).astype(jnp.bfloat16)
            query_grad_list.append(
                (
                    jnp.einsum(
                        "hqk,khd->qhd", d_scores, key_group, preferred_element_type=jnp.float32
                    )
                    * scale
                ).reshape(row_count, group_width)
            )
            log_sum_list.append(log_sum)
            delta_list.append(delta_row)
            key_grad_list.append(
                (
                    jnp.einsum(
                        "hqk,qhd->khd", d_scores, query_group, preferred_element_type=jnp.float32
                    )
                    * scale
                ).reshape(length_all, group_width)
            )
            value_grad_list.append(
                jnp.einsum(
                    "hqk,qhd->khd", probability_low, d_group, preferred_element_type=jnp.float32
                ).reshape(length_all, group_width)
            )
        d_query = jnp.concatenate(query_grad_list, axis=1).astype(jnp.bfloat16)
        d_keys_sum, d_values_sum = (
            lax.psum_scatter(
                jnp.concatenate(key_grad_list, axis=1), "seq", scatter_dimension=0, tiled=True
            ),
            lax.psum_scatter(
                jnp.concatenate(value_grad_list, axis=1), "seq", scatter_dimension=0, tiled=True
            ),
        )
        d_keys = d_keys_sum.astype(jnp.bfloat16)
        d_values = d_values_sum.astype(jnp.bfloat16)
        d_w_query = outer_product(tokens, d_query)
        d_b_query = column_sum(d_query)
        d_w_key = outer_product(tokens, d_keys)
        d_w_value = outer_product(tokens, d_values)
        d_b_value = column_sum(d_values)
        d_tokens = (
            backward_product(d_query, w_query)
            + backward_product(d_keys, w_key)
            + backward_product(d_values, w_value)
            + d_res_one
        )
        input_grad_list.append(d_tokens.astype(jnp.bfloat16))
        local_grads = jnp.concatenate(
            [
                term.ravel()
                for term in (
                    d_w_query,
                    d_w_key,
                    d_w_value,
                    d_w_out,
                    d_w_in,
                    d_w_down,
                    d_b_query,
                    d_b_value,
                    d_b_out,
                    d_gain_one,
                    d_shift_one,
                    d_b_in,
                    d_b_down,
                    d_gain_two,
                    d_shift_two,
                )
            ]
        )
        share = lax.psum_scatter(local_grads, ("batch", "seq"), scatter_dimension=0, tiled=True)
        grad_total = share if grad_total is None else grad_total + share
    return (jnp.stack(output_list)[:, None], jnp.stack(input_grad_list)[:, None], grad_total)


def solution(mesh):
    placed = (
        P(None, "batch", "seq", None),
        P(("batch", "seq")),
        P(None, "batch", None),
        P(None, "batch", "seq", None),
    )
    return jax.shard_map(
        body,
        mesh=mesh,
        in_specs=placed,
        out_specs=(
            P(None, "batch", "seq", None),
            P(None, "batch", "seq", None),
            P(("batch", "seq")),
        ),
        check_vma=False,
    )
```

profile of v0, /device:TPU:0, one launch (start us, length us, event | category | flops | bytes accessed | tf_op | source)
XLA Modules:
  0.0 1328.3 jit_solution(13397877455778654682)
XLA Ops:
  7.2 5.1 broadcast.395
  12.4 7.6 dynamic-update-slice
  20.0 252.7 %all-reduce.5.cloned.1.call-done = bf16[7087104]{0:T(1024)(128)(2,1)} async-done(((bf16[7087104]{0:T(1024)(128)(2,1)}), bf16[7087104]{0:T(1024)(128)(2,1)}) %all-reduce.5.cloned.1.call-update) | async-done | bytes 14174224
  272.8 4.2 fusion.145
  280.5 2.6 slice.251
  286.8 8.3 fusion.144
  295.1 8.3 slice.265
  304.5 2.6 slice.247
  313.6 9.3 slice.268
  329.8 2.3 fusion.147
  333.1 27.5 %all-gather.7.cloned.1.call-done = bf16[1024,768]{1,0:T(8,128)(2,1)} async-done(((bf16[64,768]{1,0:T(8,128)(2,1)}), bf16[1024,768]{1,0:T(8,128)(2,1)}) %all-gather.7.cloned.1.call-update) | async-done | bytes 1572880 | tf_op jit(solution)/shard_map/all_gather | solution.py:120
  360.6 2.5 fusion.146
  368.9 2.1 copy.101
  371.0 2.1 copy.102
  373.1 2.4 fusion.157
  376.1 25.0 %all-gather.9.cloned.1.call-done = bf16[1024,768]{1,0:T(8,128)(2,1)} async-done(((bf16[64,768]{1,0:T(8,128)(2,1)}), bf16[1024,768]{1,0:T(8,128)(2,1)}) %all-gather.9.cloned.1.call-update) | async-done | bytes 1572880 | tf_op jit(solution)/shard_map/all_gather | solution.py:121
  401.1 2.6 fusion.149
  412.3 3.6 multiply_convert_fusion.7
  418.9 22.7 %all-gather.11.cloned.1.call-done = bf16[1024,768]{1,0:T(8,128)(2,1)} async-done(((bf16[64,768]{1,0:T(8,128)(2,1)}), bf16[1024,768]{1,0:T(8,128)(2,1)}) %all-gather.11.cloned.1.call-update) | async-done | bytes 1572880 | tf_op jit(solution)/shard_map/all_gather | solution.py:120
  441.6 2.6 fusion.148
  444.2 2.0 copy.117
  446.2 2.5 fusion.160
  454.0 2.4 fusion.161
  457.6 2.0 copy.110
  463.3 2.6 exponential_reduce_fusion
  472.2 2.5 multiply_convert_fusion.6
  478.7 2.2 convert_reduce_fusion
  483.1 2.2 convert_reduce_fusion.1
  485.4 2.3 multiply_reduce_fusion.7
  505.6 3.6 copy.145
  518.8 3.8 copy.147
  524.7 2.5 multiply_reduce_fusion.1
  535.0 3.9 copy.149
  540.3 2.4 copy.151
  549.6 2.4 reshape.621
  558.3 3.1 copy.140
  561.3 3.2 reshape.627
  574.0 5.9 copy.165
  579.9 5.0 fusion.165
  584.9 11.2 reshape.626
  598.1 2.3 reshape.630
  602.0 5.7 copy.166
  607.7 5.0 fusion.166
  612.7 10.8 reshape.632
  626.8 3.2 copy.138
  629.9 3.2 reshape.622
  633.2 10.3 reduce-scatter.15.cloned.1.call-done
  646.4 3.2 copy.139
  649.5 3.2 reshape.623
  652.8 59.7 %reduce-scatter.19.cloned.1.call-done = f32[64,768]{1,0:T(8,128)} async-done(((f32[1024,768]{1,0:T(8,128)}), f32[64,768]{1,0:T(8,128)}) %reduce-scatter.19.cloned.1.call-update) | async-done | bytes 196624
  715.7 65.9 %reduce-scatter.17.cloned.1.call-done = f32[64,768]{1,0:T(8,128)} async-done(((f32[1024,768]{1,0:T(8,128)}), f32[64,768]{1,0:T(8,128)}) %reduce-scatter.17.cloned.1.call-update) | async-done | bytes 196624
  784.7 3.0 copy.141
  787.7 3.2 reshape.628
  791.0 3.0 copy.142
  794.0 3.2 reshape.629
  797.3 3.3 constant_dynamic-update-slice_fusion.26
  803.7 9.6 constant_dynamic-update-slice_fusion.20
  813.5 4.9 constant_dynamic-update-slice_fusion.18
  818.4 2.1 constant_dynamic-update-slice_fusion.16
  835.8 4.9 constant_dynamic-update-slice_fusion.21
  842.2 3.8 constant_dynamic-update-slice_fusion.19
  857.7 28.7 %add.284 = f32[7087104]{0:T(1024)} add(f32[7087104]{0:T(1024)} %constant_dynamic-update-slice_fusion, f32[7087104]{0:T(1024)} %constant_dynamic-update-slice_fusion.1) | non-fusion elementwise | flops 7087104 | bytes 85045248 | tf_op jit(solution)/shard_map/add | solution.py:278
  894.9 423.7 %all-reduce.7.cloned.1.call-done = f32[7087104]{0:T(1024)} async-done(((f32[7087104]{0:T(1024)}), f32[7087104]{0:T(1024)}) %all-reduce.7.cloned.1.call-update) | async-done | bytes 28348432
  1318.6 2.4 dynamic-slice.2
  (595 shorter events, 179.2 us)
Async XLA Ops:
  7.2 265.6 %all-reduce.5.cloned.1.call-start = ((), (), s32[]{:S(2)}) async-start(), calls=%async_computation.8 | async-start | bytes 28348416
  20.0 259.5 %copy-start.14 = (bf16[2,1,64,768]{3,2,1,0:T(8,128)(2,1)S(1)}, bf16[2,1,64,768]{3,2,1,0:T(8,128)(2,1)}, u32[]{:S(2)}) copy-start(bf16[2,1,64,768]{3,2,1,0:T(8,128)(2,1)} %param.4) | copy-start | bytes 589828
  20.0 309.8 %all-gather.5.cloned.1.call-start = ((), (), s32[]{:S(2)}) async-start(), calls=%async_computation.4 | async-start | bytes 1671168 | tf_op jit(solution)/shard_map/all_gather | solution.py:121
  278.0 17.1 %copy-start = (bf16[768,768]{1,0:T(8,128)(2,1)}, bf16[768,768]{1,0:T(8,128)(2,1)S(1)}, u32[]{:S(2)}) copy-start(bf16[768,768]{1,0:T(8,128)(2,1)S(1)} %slice.242) | copy-start | bytes 3538948
  280.4 80.1 %all-gather.7.cloned.1.call-start = ((), (), s32[]{:S(2)}) async-start(), calls=%async_computation.5 | async-start | bytes 1671168 | tf_op jit(solution)/shard_map/all_gather | solution.py:120
  283.1 43.2 %copy-start.2 = (bf16[768,768]{1,0:T(8,128)(2,1)}, bf16[768,768]{1,0:T(8,128)(2,1)S(1)}, u32[]{:S(2)}) copy-start(bf16[768,768]{1,0:T(8,128)(2,1)S(1)} %slice.251) | copy-start | bytes 3538948
  284.1 116.9 %all-gather.9.cloned.1.call-start = ((), (), s32[]{:S(2)}) async-start(), calls=%async_computation.6 | async-start | bytes 1671168 | tf_op jit(solution)/shard_map/all_gather | solution.py:121
  286.7 154.9 %all-gather.11.cloned.1.call-start = ((), (), s32[]{:S(2)}) async-start(), calls=%async_computation.7 | async-start | bytes 1671168 | tf_op jit(solution)/shard_map/all_gather | solution.py:120
  295.1 8.3 copy-start.27
  307.1 15.8 %copy-start.4 = (bf16[768,768]{1,0:T(8,128)(2,1)}, bf16[768,768]{1,0:T(8,128)(2,1)S(1)}, u32[]{:S(2)}) copy-start(bf16[768,768]{1,0:T(8,128)(2,1)S(1)} %slice.247) | copy-start | bytes 3538948
  328.2 35.1 %copy-start.73 = (pred[64,1024]{1,0:T(8,128)(4,1)S(1)}, pred[64,1024]{1,0:T(8,128)(4,1)}, u32[]{:S(2)}) copy-start(pred[64,1024]{1,0:T(8,128)(4,1)} %broadcast_compare_fusion.1) | copy-start | bytes 196612
  328.2 35.1 %copy-start.90 = (bf16[64,256]{0,1:T(8,128)(2,1)S(1)}, bf16[64,256]{0,1:T(8,128)(2,1)}, u32[]{:S(2)}) copy-start(bf16[64,256]{0,1:T(8,128)(2,1)} %copy.155) | copy-start | bytes 98308
  328.2 295.6 %reduce-scatter.13.cloned.1.call-start = ((), (), s32[]{:S(2)}) async-start(), calls=%async_computation.9 | async-start | bytes 3342336
  332.0 35.4 %copy-start.88 = (bf16[64,256]{0,1:T(8,128)(2,1)S(1)}, bf16[64,256]{0,1:T(8,128)(2,1)}, u32[]{:S(2)}) copy-start(bf16[64,256]{0,1:T(8,128)(2,1)} %copy.154) | copy-start | bytes 98308
  363.1 10.0 copy-start.86
  367.4 38.2 %copy-start.123 = (f32[4,64]{1,0:T(4,128)S(1)}, f32[4,64]{1,0:T(4,128)}, u32[]{:S(2)}) copy-start(f32[4,64]{1,0:T(4,128)} %copy-done.122) | copy-start | bytes 3076
  368.9 37.8 %copy-start.116 = (f32[4,64]{1,0:T(4,128)}, f32[4,64]{1,0:T(4,128)S(1)}, u32[]{:S(2)}) copy-start(f32[4,64]{1,0:T(4,128)S(1)} %get-tuple-element.114) | copy-start | bytes 3076
  368.9 37.8 %copy-start.124 = (f32[4,64]{1,0:T(4,128)S(1)}, f32[4,64]{1,0:T(4,128)}, u32[]{:S(2)}) copy-start(f32[4,64]{1,0:T(4,128)} %copy-done.122) | copy-start | bytes 3076
  375.5 31.3 %copy-start.119 = (f32[4,64]{1,0:T(4,128)}, f32[4,64]{1,0:T(4,128)S(1)}, u32[]{:S(2)}) copy-start(f32[4,64]{1,0:T(4,128)S(1)} %get-tuple-element.116) | copy-start | bytes 3076
  415.9 30.3 %copy-start.72 = (pred[64,1024]{1,0:T(8,128)(4,1)S(1)}, pred[64,1024]{1,0:T(8,128)(4,1)}, u32[]{:S(2)}) copy-start(pred[64,1024]{1,0:T(8,128)(4,1)} %broadcast_compare_fusion) | copy-start | bytes 196612
  471.9 16.5 %copy-start.25 = (f32[64,768]{1,0:T(8,128)}, f32[64,768]{1,0:T(8,128)S(1)}, u32[]{:S(2)}) copy-start(f32[64,768]{1,0:T(8,128)S(1)} %get-tuple-element.130) | copy-start | bytes 589828
  471.9 16.5 %copy-start.133 = (f32[64]{0:T(128)}, f32[64]{0:T(128)S(1)}, u32[]{:S(2)}) copy-start(f32[64]{0:T(128)S(1)} %broadcast_multiply_fusion.1) | copy-start | bytes 772
  472.1 16.2 %copy-start.151 = (f32[64]{0:T(128)}, f32[64]{0:T(128)S(1)}, u32[]{:S(2)}) copy-start(f32[64]{0:T(128)S(1)} %fusion.122) | copy-start | bytes 772
  485.4 7.9 copy-start.118
  485.4 10.1 copy-start.121
  487.7 12.5 copy-start.91
  491.2 9.8 copy-start.78
  509.2 134.3 %reduce-scatter.15.cloned.1.call-start = ((), (), s32[]{:S(2)}) async-start(), calls=%async_computation.10 | async-start | bytes 3342336
  527.2 185.3 %reduce-scatter.19.cloned.1.call-start = ((), (), s32[]{:S(2)}) async-start(), calls=%async_computation.12 | async-start | bytes 3342336
  544.1 79.4 %copy-start.66 = (bf16[4,64,64]{2,1,0:T(8,128)(2,1)}, bf16[4,64,64]{2,1,0:T(8,128)(2,1)S(1)}, u32[]{:S(2)}) copy-start(bf16[4,64,64]{2,1,0:T(8,128)(2,1)S(1)} %fusion.20) | copy-start | bytes 98308
  545.6 77.8 %copy-start.67 = (bf16[4,64,64]{2,1,0:T(8,128)(2,1)}, bf16[4,64,64]{2,1,0:T(8,128)(2,1)S(1)}, u32[]{:S(2)}) copy-start(bf16[4,64,64]{2,1,0:T(8,128)(2,1)S(1)} %fusion.19) | copy-start | bytes 98308
  547.2 76.3 %copy-start.68 = (bf16[4,64,64]{2,1,0:T(8,128)(2,1)}, bf16[4,64,64]{2,1,0:T(8,128)(2,1)S(1)}, u32[]{:S(2)}) copy-start(bf16[4,64,64]{2,1,0:T(8,128)(2,1)S(1)} %fusion.18) | copy-start | bytes 98308
  553.3 70.3 %copy-start.69 = (bf16[4,64,64]{2,1,0:T(8,128)(2,1)}, bf16[4,64,64]{2,1,0:T(8,128)(2,1)S(1)}, u32[]{:S(2)}) copy-start(bf16[4,64,64]{2,1,0:T(8,128)(2,1)S(1)} %fusion.23) | copy-start | bytes 98308
  554.9 68.8 %copy-start.70 = (bf16[4,64,64]{2,1,0:T(8,128)(2,1)}, bf16[4,64,64]{2,1,0:T(8,128)(2,1)S(1)}, u32[]{:S(2)}) copy-start(bf16[4,64,64]{2,1,0:T(8,128)(2,1)S(1)} %fusion.22) | copy-start | bytes 98308
  556.4 67.2 %copy-start.71 = (bf16[4,64,64]{2,1,0:T(8,128)(2,1)}, bf16[4,64,64]{2,1,0:T(8,128)(2,1)S(1)}, u32[]{:S(2)}) copy-start(bf16[4,64,64]{2,1,0:T(8,128)(2,1)S(1)} %fusion.21) | copy-start | bytes 98308
  564.6 217.0 %reduce-scatter.17.cloned.1.call-start = ((), (), s32[]{:S(2)}) async-start(), calls=%async_computation.11 | async-start | bytes 3342336
  566.2 752.4 %all-reduce.7.cloned.1.call-start = ((), (), s32[]{:S(2)}) async-start(), calls=%async_computation.13 | async-start | bytes 56696832
  584.8 11.2 copy-start.80
  584.8 11.2 copy-start.100
  584.8 11.2 copy-start.102
  584.9 11.2 copy-start.104
  624.9 8.2 copy-start.63
  644.5 69.1 %copy-start.43 = (bf16[64,768]{0,1:T(8,128)(2,1)}, bf16[64,768]{0,1:T(8,128)(2,1)S(1)}, u32[]{:S(2)}) copy-start(bf16[64,768]{0,1:T(8,128)(2,1)S(1)} %copy.148) | copy-start | bytes 294916
  713.6 74.1 %copy-start.45 = (bf16[64,768]{0,1:T(8,128)(2,1)}, bf16[64,768]{0,1:T(8,128)(2,1)S(1)}, u32[]{:S(2)}) copy-start(bf16[64,768]{0,1:T(8,128)(2,1)S(1)} %copy.152) | copy-start | bytes 294916
  782.7 8.3 copy-start.65
  802.1 11.2 slice-start.14
  803.7 9.7 slice-start.15
  803.7 9.7 slice-start.16
  813.4 8.5 copy-start.140
  813.4 9.8 copy-start.147
  813.4 11.1 copy-start.146
  813.4 12.4 copy-start.106
  813.4 13.7 %copy-start.139 = (f32[768]{0:T(1024)S(1)}, f32[768]{0:T(1024)}, u32[]{:S(2)}) copy-start(f32[768]{0:T(1024)} %get-tuple-element.44) | copy-start | bytes 9220
  813.4 15.0 %copy-start.138 = (f32[768]{0:T(1024)S(1)}, f32[768]{0:T(1024)}, u32[]{:S(2)}) copy-start(f32[768]{0:T(1024)} %get-tuple-element.28) | copy-start | bytes 9220
  813.4 16.3 %copy-start.143 = (f32[768]{0:T(1024)S(1)}, f32[768]{0:T(1024)}, u32[]{:S(2)}) copy-start(f32[768]{0:T(1024)} %get-tuple-element.35) | copy-start | bytes 9220
  813.4 17.5 %copy-start.18 = (f32[589824]{0:T(1024)S(1)}, f32[589824]{0:T(1024)}, u32[]{:S(2)}) copy-start(f32[589824]{0:T(1024)} %reshape.628) | copy-start | bytes 7077892
  813.4 22.3 %slice-start.8 = ((s8[9437184]{0:T(1024)(128)(4,1)}), s8[4194304]{0:T(1024)(128)(4,1)S(1)}, s32[]{:S(2)}) async-start(s8[9437184]{0:T(1024)(128)(4,1)} %bitcast.330), calls=%async_computation.22 | async-start | bytes 8388608
  813.5 22.3 %slice-start.9 = ((s8[9437184]{0:T(1024)(128)(4,1)}), s8[4194304]{0:T(1024)(128)(4,1)S(1)}, s32[]{:S(2)}) async-start(s8[9437184]{0:T(1024)(128)(4,1)} %bitcast.330), calls=%async_computation.23 | async-start | bytes 8388608
  818.4 14.1 %copy-start.19 = (f32[589824]{0:T(1024)S(1)}, f32[589824]{0:T(1024)}, u32[]{:S(2)}) copy-start(f32[589824]{0:T(1024)} %reshape.629) | copy-start | bytes 7077892
  842.2 9.0 copy-start.144
  842.2 10.4 copy-start.105
  842.2 11.7 copy-start.137
  842.2 13.0 copy-start.136
  842.2 14.2 %copy-start.142 = (f32[768]{0:T(1024)S(1)}, f32[768]{0:T(1024)}, u32[]{:S(2)}) copy-start(f32[768]{0:T(1024)} %get-tuple-element.34) | copy-start | bytes 9220
  (137 other events, 508.5 us)
Sparse Core Ops, SparseCore 0:
  20.1 252.6 all-reduce.4
  280.6 38.7 all-gather.4
  322.2 38.2 all-gather.6
  362.7 38.2 all-gather.8
  403.2 38.3 all-gather.10
  509.3 65.0 reduce-scatter.12
  578.2 65.2 reduce-scatter.14
  647.2 65.2 reduce-scatter.18
  716.3 65.2 reduce-scatter.16
  886.5 432.0 all-reduce.6
where the time goes:
time: 1340 us; the launch traced here: 1330 us
  waiting for transfers between devices  888 us (66%)
  local copies, waits for them, and re-layouts  259 us (19%)
  matrix products  96.9 us (7%)
  other arithmetic  67.2 us (5%)
  between operations  17.1 us (1%)
    unnamed x16, waiting for transfers between devices  812 us
    unnamed x423, local copies, waits for them, and re-layouts  114 us
    all_gather x2, waiting for transfers between devices, body(): lax.all_gather(keys_own, 'seq', axis=0, tiled=True)  50.2 us
    reshape x10, local copies, waits for them, and re-layouts, body(): term.ravel()  44.4 us
    slice x8, local copies, waits for them, and re-layouts, unpack_params(): pieces_list.append(flat_params[offset:offset + entry_count].reshape(extent))  37.4 us
    add x1, other arithmetic, body(): grad_total = share if grad_total is None else grad_total + share  28.7 us
  transfers between devices with their start and end apart: 10, of which 8 were waited for; matrix products, arithmetic and copies ran while one was open for 17% of the time, Pallas kernels for 0%

commit v1 on v0

v1 whole, which is shorter than its diff:
```python
import math
from functools import partial

import jax
import jax.numpy as jnp
from jax import lax
from jax.experimental import pallas as pl
from jax.experimental.pallas import tpu as pltpu
from jax.sharding import PartitionSpec as P

D = 768
HD = 64
FF = 3072
HEADS = 12
GROUP = 4
GW = GROUP * HD
AUX = 128
TILE = 16
epsilon = 1e-12
ALL = ("batch", "seq")
f32 = jnp.float32
bf16 = jnp.bfloat16
NEG = -1e30


def project(a, b):
    return jnp.dot(a, b, preferred_element_type=f32)


def outer_product(a, b):
    return lax.dot_general(a, b, (((0,), (0,)), ((), ())), preferred_element_type=f32)


def backward_product(a, b):
    return lax.dot_general(a, b, (((1,), (1,)), ((), ())), preferred_element_type=f32)


def stack_heads(block):
    lane = lax.broadcasted_iota(jnp.int32, block.shape, 1) // HD
    zero = jnp.zeros_like(block)
    return jnp.concatenate([jnp.where(lane == h, block, zero) for h in range(GROUP)], axis=0)


def unstack_heads(stacked, rows):
    lane = lax.broadcasted_iota(jnp.int32, (rows, GW), 1) // HD
    total = stacked[:rows]
    for h in range(1, GROUP):
        total = jnp.where(lane == h, stacked[h * rows : (h + 1) * rows], total)
    return total


def flat_rows(ref):
    value = ref[...]
    return value.reshape(-1, value.shape[-1])


def nt(a, b):
    return lax.dot_general(a, b, (((1,), (1,)), ((), ())), preferred_element_type=f32)


def forward_kernel(q_ref, k_ref, v_ref, sq_ref, sk_ref, o_ref, aux_ref):
    group = pl.program_id(1)
    q = q_ref[0]
    rows = q.shape[0]
    keys, values = flat_rows(k_ref), flat_rows(v_ref)
    same = sq_ref[0] == sk_ref[0]
    scores = nt(stack_heads(q), keys) * (HD**-0.5)
    lane = lax.broadcasted_iota(jnp.int32, (rows, AUX), 1)
    probs, aux = [], jnp.zeros((rows, AUX), f32)
    for h in range(GROUP):
        masked = jnp.where(same, scores[h * rows : (h + 1) * rows], NEG)
        top = jnp.max(masked, axis=1, keepdims=True)
        weight = jnp.exp(masked - top)
        total = jnp.sum(weight, axis=1, keepdims=True)
        probs.append((weight / total).astype(bf16))
        head = group * GROUP + h
        aux = aux + jnp.where((lane % 32 == head) & (lane < 96), top + jnp.log(total), 0.0)
    mixed = jnp.dot(jnp.concatenate(probs, axis=0), values, preferred_element_type=f32)
    o_ref[0] = unstack_heads(mixed, rows)

    @pl.when(group == 0)
    def _():
        aux_ref[0] = aux

    @pl.when(group > 0)
    def _():
        aux_ref[0] = aux_ref[0] + aux


def pack_kernel(da_ref, o_ref, aux_ref, out_ref):
    da = da_ref[...].astype(bf16)
    prod = da.astype(f32) * o_ref[...]
    head = lax.broadcasted_iota(jnp.int32, (D, AUX), 0) // HD
    lane_c = lax.broadcasted_iota(jnp.int32, (D, AUX), 1)
    select = jnp.where((lane_c % 32 == head + HEADS) & (lane_c < 96), 1.0, 0.0).astype(f32)
    delta = jnp.dot(prod, select, precision=lax.Precision.HIGHEST, preferred_element_type=f32)
    both = aux_ref[...] + delta
    lane = lax.broadcasted_iota(jnp.int32, both.shape, 1)
    high = both.astype(bf16).astype(f32)
    rest = both - high
    middle = rest.astype(bf16).astype(f32)
    low = rest - middle
    out_ref[:, :D] = da
    out_ref[:, D:] = jnp.where(lane < 32, high, jnp.where(lane < 64, middle, low)).astype(bf16)


def query_grad_kernel(q_ref, k_ref, v_ref, da_ref, sq_ref, sk_ref, dq_ref):
    q = q_ref[0]
    rows = q.shape[0]
    keys, values = flat_rows(k_ref), flat_rows(v_ref)
    same = sq_ref[0] == sk_ref[0]
    scores = nt(stack_heads(q), keys) * (HD**-0.5)
    d_prob = nt(stack_heads(da_ref[0]), values)
    parts = []
    for h in range(GROUP):
        masked = jnp.where(same, scores[h * rows : (h + 1) * rows], NEG)
        weight = jnp.exp(masked - jnp.max(masked, axis=1, keepdims=True))
        prob = weight / jnp.sum(weight, axis=1, keepdims=True)
        dp = d_prob[h * rows : (h + 1) * rows]
        delta = jnp.sum(prob * dp, axis=1, keepdims=True)
        parts.append((prob * (dp - delta)).astype(bf16))
    mixed = jnp.dot(jnp.concatenate(parts, axis=0), keys, preferred_element_type=f32)
    dq_ref[0] = (unstack_heads(mixed, rows) * (HD**-0.5)).astype(bf16)


def key_grad_kernel(k_ref, v_ref, q_ref, da_ref, aux_ref, sk_ref, sq_ref, dk_ref, dv_ref):
    group = pl.program_id(1)
    k = k_ref[0]
    rows = k.shape[0]
    queries, d_att, aux = flat_rows(q_ref), flat_rows(da_ref), flat_rows(aux_ref)
    same = sk_ref[0] == sq_ref[0]
    row = lax.broadcasted_iota(jnp.int32, (2 * GROUP, AUX), 0)
    lane = lax.broadcasted_iota(jnp.int32, (2 * GROUP, AUX), 1)
    wanted = group * GROUP + row % GROUP + HEADS * (row // GROUP)
    select = jnp.where((lane % 32 == wanted) & (lane < 96), 1.0, 0.0).astype(bf16)
    stats = nt(select, aux)
    scores = nt(stack_heads(k), queries) * (HD**-0.5)
    d_prob = nt(stack_heads(v_ref[0]), d_att)
    probs, parts = [], []
    for h in range(GROUP):
        masked = jnp.where(same, scores[h * rows : (h + 1) * rows], NEG)
        prob = jnp.exp(masked - stats[h : h + 1])
        dp = d_prob[h * rows : (h + 1) * rows]
        probs.append(prob.astype(bf16))
        parts.append((prob * (dp - stats[GROUP + h : GROUP + h + 1])).astype(bf16))
    d_key = jnp.dot(jnp.concatenate(parts, axis=0), queries, preferred_element_type=f32)
    d_value = jnp.dot(jnp.concatenate(probs, axis=0), d_att, preferred_element_type=f32)
    dk_ref[0] = (unstack_heads(d_key, rows) * (HD**-0.5)).astype(bf16)
    dv_ref[0] = unstack_heads(d_value, rows).astype(bf16)


def own_spec(rows):
    return pl.BlockSpec((1, rows, GW), lambda m, g: (m, 0, g))


def all_spec(count, rows):
    return pl.BlockSpec((count, None, rows, GW), lambda m, g: (0, m, 0, g))


def column_spec(rows):
    return pl.BlockSpec((1, rows, 1), lambda m, g: (m, 0, 0))


def row_spec(length):
    return pl.BlockSpec((1, 1, length), lambda m, g: (m, 0, 0))


def attention_forward(q, k, v, seg_own, seg_all):
    micro, rows, _ = q.shape
    count, length = k.shape[0], seg_all.shape[-1]
    cost = pl.CostEstimate(
        flops=2 * micro * 3 * 2 * GW * length * GW,
        bytes_accessed=4 * k.size,
        transcendentals=micro * HEADS * rows * length,
    )
    return pl.pallas_call(
        forward_kernel,
        grid=(micro, D // GW),
        in_specs=[
            own_spec(rows),
            all_spec(count, rows),
            all_spec(count, rows),
            column_spec(rows),
            row_spec(length),
        ],
        out_specs=[own_spec(rows), pl.BlockSpec((1, rows, AUX), lambda m, g: (m, 0, 0))],
        out_shape=[
            jax.ShapeDtypeStruct((micro, rows, D), f32),
            jax.ShapeDtypeStruct((micro, rows, AUX), f32),
        ],
        cost_estimate=cost,
        name="attend",
    )(q, k, v, seg_own, seg_all)


def pack_gradient(d_att, mixed, aux):
    return pl.pallas_call(
        pack_kernel,
        out_shape=jax.ShapeDtypeStruct((d_att.shape[0], D + AUX), bf16),
        name="pack",
    )(d_att, mixed, aux)


def attention_query_grad(q, k, v, packed, seg_own, seg_all):
    micro, rows, _ = q.shape
    count, length = k.shape[0], seg_all.shape[-1]
    cost = pl.CostEstimate(
        flops=3 * micro * 3 * 2 * GW * length * GW,
        bytes_accessed=4 * k.size,
        transcendentals=micro * HEADS * rows * length,
    )
    return pl.pallas_call(
        query_grad_kernel,
        grid=(micro, D // GW),
        in_specs=[
            own_spec(rows),
            all_spec(count, rows),
            all_spec(count, rows),
            own_spec(rows),
            column_spec(rows),
            row_spec(length),
        ],
        out_specs=own_spec(rows),
        out_shape=jax.ShapeDtypeStruct((micro, rows, D), bf16),
        cost_estimate=cost,
        name="query_grad",
    )(q, k, v, packed, seg_own, seg_all)


def attention_key_grad(k, v, q, packed, seg_own, seg_all):
    micro, rows, _ = k.shape
    count, length = q.shape[0], seg_all.shape[-1]
    cost = pl.CostEstimate(
        flops=4 * micro * 3 * 2 * GW * length * GW,
        bytes_accessed=4 * q.size,
        transcendentals=micro * HEADS * rows * length,
    )
    return pl.pallas_call(
        key_grad_kernel,
        grid=(micro, D // GW),
        in_specs=[
            own_spec(rows),
            own_spec(rows),
            all_spec(count, rows),
            all_spec(count, rows),
            pl.BlockSpec((count, None, rows, AUX), lambda m, g: (0, m, 0, D // AUX)),
            column_spec(rows),
            row_spec(length),
        ],
        out_specs=[own_spec(rows), own_spec(rows)],
        out_shape=[jax.ShapeDtypeStruct((micro, rows, D), bf16)] * 2,
        cost_estimate=cost,
        name="key_grad",
    )(k, v, q, packed, packed, seg_own, seg_all)


class Plan:
    def __init__(self, shard, devices):
        total = shard * devices
        assert total % D == 0
        self.shard, self.devices, self.rows = shard, devices, total // D
        self.base = [d * shard // D // TILE * TILE for d in range(devices)]
        ends = [-(-(d + 1) * shard // D) for d in range(devices)]
        need = max(e - b for e, b in zip(ends, self.base))
        self.block = -(-need // TILE) * TILE
        self.offset = [d * shard - b * D for d, b in enumerate(self.base)]

    def place(self, flat, me):
        offset = me * self.shard - me * self.shard // D // TILE * TILE * D
        wide = jnp.zeros((self.block * D,), flat.dtype)
        wide = lax.dynamic_update_slice(wide, flat, (offset,))
        return wide.reshape(self.block, D)

    def take(self, block, me):
        offset = me * self.shard - me * self.shard // D // TILE * TILE * D
        return lax.dynamic_slice(block.reshape(-1), (offset,), (self.shard,))

    def assemble(self, blocks, first, last):
        marks = {first, last}
        for b in self.base:
            for m in (b, b + self.block):
                if first < m < last:
                    marks.add(m)
        marks = sorted(marks)
        pieces = []
        for a, z in zip(marks, marks[1:]):
            parts = [
                blocks[d][a - b : z - b]
                for d, b in enumerate(self.base)
                if b <= a and z <= b + self.block
            ]
            piece = parts[0]
            for part in parts[1:]:
                piece = piece + part
            pieces.append(piece)
        return pieces[0] if len(pieces) == 1 else jnp.concatenate(pieces, axis=0)

    def cut(self, matrices):
        blocks = []
        for b in self.base:
            pieces, at, end = [], 0, b + self.block
            for matrix in matrices:
                rows = matrix.shape[0]
                lo, hi = max(b, at), min(end, at + rows)
                if lo < hi:
                    pieces.append(matrix[lo - at : hi - at])
                at += rows
            if end > at:
                pieces.append(jnp.zeros((end - max(at, b), D), matrices[0].dtype))
            blocks.append(pieces[0] if len(pieces) == 1 else jnp.concatenate(pieces, axis=0))
        return jnp.stack(blocks)


def norm(values):
    average = jnp.mean(values, axis=-1, keepdims=True)
    centred = values - average
    variance = jnp.mean(centred * centred, axis=-1, keepdims=True)
    inverse = lax.rsqrt(variance + epsilon)
    return centred * inverse, inverse


def norm_back(gradient, normed, inverse):
    mean_one = jnp.mean(gradient, axis=-1, keepdims=True)
    mean_two = jnp.mean(gradient * normed, axis=-1, keepdims=True)
    return inverse * (gradient - mean_one - normed * mean_two)


def column_sum(matrix):
    return jnp.sum(matrix.astype(f32), axis=0)


def body(seq_count, batch_count, inputs, params, segment_ids, cotangent):
    micro, _, rows, _ = inputs.shape
    tokens = micro * rows
    plan = Plan(params.shape[0], seq_count * batch_count)
    place_seq = lax.axis_index("seq")
    me = lax.axis_index("batch") * seq_count + place_seq
    length = segment_ids.shape[-1]

    x_own = inputs[:, 0]
    x_flat = x_own.reshape(tokens, D)
    x_all = lax.all_gather(x_own, "seq", axis=0, tiled=False)
    blocks = lax.all_gather(plan.place(params, me), ALL, axis=0, tiled=False)

    def matrix(first, count):
        return plan.assemble(blocks, first, first + count)

    w_query, w_key, w_value, w_out = (matrix(i * D, D) for i in range(4))
    w_in = matrix(4 * D, FF).reshape(D, FF)
    w_down = matrix(4 * D + FF, FF)
    vectors = matrix(4 * D + 2 * FF, 12).astype(f32)
    b_query, b_value, b_out, gain_one, shift_one = (vectors[i] for i in range(5))
    b_in = vectors[5:9].reshape(FF)
    b_down, gain_two, shift_two = (vectors[i] for i in range(9, 12))

    seg = segment_ids[:, 0]
    seg_own = lax.dynamic_slice_in_dim(seg, place_seq * rows, rows, axis=1)[:, :, None]
    seg_all = seg[:, None, :]

    x_rows = x_all.reshape(-1, D)
    split = (seq_count, micro, rows, D)
    q_all = (project(x_rows, w_query) + b_query).astype(bf16).reshape(split)
    k_all = project(x_rows, w_key).astype(bf16).reshape(split)
    v_all = (project(x_rows, w_value) + b_value).astype(bf16).reshape(split)
    q_own, k_own, v_own = (
        lax.dynamic_index_in_dim(a, place_seq, 0, keepdims=False) for a in (q_all, k_all, v_all)
    )

    mixed, aux = attention_forward(q_own, k_all, v_all, seg_own, seg_all)
    mixed = mixed.reshape(tokens, D)
    aux = aux.reshape(tokens, AUX)
    attended = mixed.astype(bf16)
    res_one = x_flat.astype(f32) + project(attended, w_out) + b_out
    n_one, r_one = norm(res_one)
    first_norm = n_one * gain_one + shift_one
    first_low = first_norm.astype(bf16)
    inner = project(first_low, w_in) + b_in
    phi_cdf = 0.5 * (1.0 + lax.erf(inner * math.sqrt(0.5)))
    hidden = (inner * phi_cdf).astype(bf16)
    res_two = first_norm + project(hidden, w_down) + b_down
    n_two, r_two = norm(res_two)
    outputs = (n_two * gain_two + shift_two).astype(bf16)

    grad = cotangent[:, 0].reshape(tokens, D).astype(f32)
    d_gain_two = column_sum(grad * n_two)
    d_shift_two = column_sum(grad)
    d_res_two = norm_back(grad * gain_two, n_two, r_two)
    d_second = d_res_two.astype(bf16)
    slope = phi_cdf + inner * (jnp.exp(-0.5 * inner * inner) * (1.0 / math.sqrt(2.0 * math.pi)))
    d_inner = (backward_product(d_second, w_down) * slope).astype(bf16)
    d_first = d_res_two + backward_product(d_inner, w_in)
    d_gain_one = column_sum(d_first * n_one)
    d_shift_one = column_sum(d_first)
    d_res_one = norm_back(d_first * gain_one, n_one, r_one)
    d_branch = d_res_one.astype(bf16)
    d_att = backward_product(d_branch, w_out)

    packed = pack_gradient(d_att, mixed, aux).reshape(micro, rows, D + AUX)
    packed_all = lax.all_gather(packed, "seq", axis=0, tiled=False)
    d_query = attention_query_grad(q_own, k_all, v_all, packed, seg_own, seg_all)
    d_query = d_query.reshape(tokens, D)
    d_w_down = outer_product(hidden, d_second).astype(bf16)
    d_w_in = outer_product(first_low, d_inner).astype(bf16)
    d_w_out = outer_product(attended, d_branch).astype(bf16)

    d_keys, d_values = attention_key_grad(k_own, v_own, q_all, packed_all, seg_own, seg_all)
    d_keys = d_keys.reshape(tokens, D)
    d_values = d_values.reshape(tokens, D)
    d_w_query = outer_product(x_flat, d_query).astype(bf16)
    d_w_key = outer_product(x_flat, d_keys).astype(bf16)
    d_w_value = outer_product(x_flat, d_values).astype(bf16)
    d_tokens = (
        backward_product(d_query, w_query)
        + backward_product(d_keys, w_key)
        + backward_product(d_values, w_value)
        + d_res_one
    ).astype(bf16)

    d_vectors = jnp.concatenate(
        [
            column_sum(d_query)[None],
            column_sum(d_values)[None],
            column_sum(d_branch)[None],
            d_gain_one[None],
            d_shift_one[None],
            column_sum(d_inner).reshape(4, D),
            column_sum(d_second)[None],
            d_gain_two[None],
            d_shift_two[None],
        ],
        axis=0,
    ).astype(bf16)
    cut = plan.cut(
        [d_w_query, d_w_key, d_w_value, d_w_out, d_w_in.reshape(FF, D), d_w_down, d_vectors]
    )
    mine = lax.psum_scatter(cut, ALL, scatter_dimension=0, tiled=False)
    share = plan.take(mine.astype(f32), me)
    shape = (micro, 1, rows, D)
    return outputs.reshape(shape), d_tokens.reshape(shape), share


def solution(mesh):
    token_spec = P(None, "batch", "seq", None)
    return jax.shard_map(
        partial(body, mesh.shape["seq"], mesh.shape["batch"]),
        mesh=mesh,
        in_specs=(token_spec, P(ALL), P(None, "batch", None), token_spec),
        out_specs=(token_spec, token_spec, P(ALL)),
        check_vma=False,
    )
```

time: 1340 us -> 531 us (0.40)
  waiting for transfers between devices: 888 us -> 269 us
  local copies, waits for them, and re-layouts: 259 us -> 136 us
  matrix products: 96.9 us -> 48 us
  other arithmetic: 67.2 us -> 30.5 us
  Pallas kernels: 0 us -> 29 us
    unnamed x16 -> x4, waiting for transfers between devices: 812 us -> 0.75 us
    reduce_scatter x0 -> x1, waiting for transfers between devices: none -> 162 us  [body(): mine = lax.psum_scatter(cut, ALL, scatter_dimension=0, tiled=False)]
    slice x29 -> x21, local copies, waits for them, and re-layouts: 69.3 us -> 8.4 us  [the longest x19 8.33 us: cut(): pieces.append(matrix[lo - at:hi - at])]
    unnamed x423 -> x121, local copies, waits for them, and re-layouts: 114 us -> 62.2 us
    dot_general x72 -> x18, matrix products: 96.9 us -> 48 us  [the longest x6 28.1 us: project(): return jnp.dot(a, b, preferred_element_type=f32)]
    reshape x22 -> x2, local copies, waits for them, and re-layouts: 55.3 us -> 8.48 us  [the longest x1 8.47 us: body(): w_in = matrix(4 * D, FF).reshape(D, FF)]
    all_gather x4 -> x3, waiting for transfers between devices: 75.2 us -> 106 us  [the longest x1 106 us: body(): blocks = lax.all_gather(plan.place(params, me), ALL, axis=0, tiled=False)]
    add x7 -> x0, other arithmetic: 30.7 us -> none  [the longest x1 28.7 us: body(): grad_total = share if grad_total is None else grad_total + share]
  transfers between devices with their start and end apart: 10 -> 4, of which waited for: 8 -> 2; matrix products, arithmetic and copies ran while one was open for 17% -> 18% of each run, Pallas kernels for 0% -> 2%
where the time goes in v1:
time: 531 us; the launch traced here: 527 us
  waiting for transfers between devices  269 us (51%)
  local copies, waits for them, and re-layouts  136 us (26%)
  matrix products  48 us (9%)
  other arithmetic  30.5 us (6%)
  Pallas kernels  29 us (5%)
  between operations  14.4 us (3%)
    reduce_scatter x1, waiting for transfers between devices, body(): mine = lax.psum_scatter(cut, ALL, scatter_dimension=0, tiled=False)  162 us
    all_gather x1, waiting for transfers between devices, body(): blocks = lax.all_gather(plan.place(params, me), ALL, axis=0, tiled=False)  106 us
    unnamed x121, local copies, waits for them, and re-layouts  62.2 us
    dot_general x6, matrix products, project(): return jnp.dot(a, b, preferred_element_type=f32)  28.1 us
    unnamed x21, other arithmetic  25.9 us
    another operation x11, local copies, waits for them, and re-layouts, cut(): return jnp.stack(blocks)  19.8 us
    dot_general x6, matrix products, backward_product(): lax.dot_general(a, b, (((1,), (1,)), ((), ())), preferred_element_type=f32)  10.9 us
  transfers between devices with their start and end apart: 4, of which 2 were waited for; matrix products, arithmetic and copies ran while one was open for 18% of the time, Pallas kernels for 2%

profile of v1, /device:TPU:0, one launch (start us, length us, event | category | flops | bytes accessed | tf_op | source)
XLA Modules:
  0.0 526.8 jit_solution(1675518066064671203)
XLA Ops:
  7.3 7.2 %dynamic_update_slice.3 = bf16[233472]{0:T(1024)(128)(2,1)S(1)} dynamic-update-slice(bf16[233472]{0:T(1024)(128)(2,1)S(1)} %broadcast_in_dim.49, bf16[221472]{0:T(1024)(128)(2,1)} %param.5, s32[]{:T(128)S(6)} %select_n.25) | dynamic-update-slice | bytes 885892 | tf_op jit(solution)/shard_map/dynamic_update_slice | solution.py:271
  18.0 106.4 %all-gather.5.cloned.1.call-done = bf16[32,304,768]{2,1,0:T(8,128)(2,1)} async-done(((bf16[1,304,768]{2,1,0:T(8,128)(2,1)}), bf16[32,304,768]{2,1,0:T(8,128)(2,1)}) %all-gather.5.cloned.1.call-update) | async-done | bytes 14942224 | tf_op jit(solution)/shard_map/all_gather | solution.py:343
  124.4 1.7 constant_dynamic-update-slice_fusion.24
  127.5 1.8 fusion.56
  130.6 1.8 fusion.55
  133.8 1.8 fusion.54
  137.0 1.8 fusion.53
  138.8 1.8 fusion.73
  142.0 2.1 fusion.52
  145.5 2.1 fusion.51
  149.1 2.1 fusion.50
  151.2 1.4 constant_dynamic-update-slice_fusion.16
  152.6 2.1 fusion.49
  154.7 1.5 constant_dynamic-update-slice_fusion.15
  157.3 2.5 fusion.48
  159.8 1.6 constant_dynamic-update-slice_fusion.14
  161.3 2.8 fusion.47
  164.1 1.6 constant_dynamic-update-slice_fusion.13
  166.7 1.7 constant_dynamic-update-slice_fusion.12
  168.4 8.5 %reshape.288 = bf16[768,3072]{1,0:T(8,128)(2,1)} reshape(bf16[3072,768]{1,0:T(8,128)(2,1)} %get-tuple-element.35) | data formatting | bytes 9437184 | tf_op jit(solution)/shard_map/reshape | solution.py:349
  178.8 7.0 %fusion.2 = bf16[2048,768]{0,1:T(8,128)(2,1)} fusion(f32[768]{0:T(1024)S(1)} %get-tuple-element.30, bf16[768,768]{1,0:T(8,128)(2,1)S(1)} %get-tuple-element.85, bf16[2048,768]{1,0:T(8,128)(2,1)} %bitcast.464), kind=kOutput, calls=%fused_computation.9 | convolution fusion | flops 2419064832 | bytes 7474176 | tf_op jit(solution)/shard_map/dot_general | solution.py:27
  185.8 4.7 copy.15
  190.5 6.6 %fusion.1 = bf16[2048,768]{0,1:T(8,128)(2,1)} fusion(bf16[768,768]{1,0:T(8,128)(2,1)} %get-tuple-element.36, bf16[2048,768]{1,0:T(8,128)(2,1)} %bitcast.465), kind=kOutput, calls=%fused_computation.8 | convolution fusion | flops 2417491968 | bytes 7471104 | tf_op jit(solution)/shard_map/dot_general | solution.py:27
  197.1 4.8 copy.16
  201.9 1.8 fusion.40
  205.1 1.8 fusion.39
  208.2 2.0 fusion.59
  210.2 6.6 %fusion.3 = bf16[2048,768]{0,1:T(8,128)(2,1)} fusion(f32[768]{0:T(1024)S(1)} %get-tuple-element.29, bf16[768,768]{1,0:T(8,128)(2,1)S(1)} %get-tuple-element.81, bf16[2048,768]{1,0:T(8,128)(2,1)} %bitcast.466), kind=kOutput, calls=%fused_computation.10 | convolution fusion | flops 2419064832 | bytes 7474176 | tf_op jit(solution)/shard_map/dot_general | solution.py:27
  216.8 4.7 copy.17
  221.5 1.7 dynamic-slice_bitcast_fusion.2.q_ref
  223.1 8.8 %attend.1 = (f32[2,64,768]{2,1,0:T(8,128)}, f32[2,64,128]{2,1,0:T(8,128)}) custom-call(bf16[2,64,768]{2,1,0:T(8,128)(2,1)} %dynamic-slice_bitcast_fusion.2.q_ref, bf16[16,2,64,768]{3,2,1,0:T(8,128)(2,1)} %bitcast.437, bf16[16,2,64,768]{3,2,1,0:T(8,128)(2,1)} %bitcast.440, s32[2,64,1]{2,1,0:T(8,128)} %copy.18.sq_ref.sk_ref, s32[2,1,1024]{2,1,0:T(1,128)} %sq_ref.1), custom_call_target="tpu_custom_call" | custom-call | flops 1610612736 | bytes 6291456 | tf_op jit(solution)/shard_map/attend/pallas_call | solution.py:176
  233.6 3.2 convolution_add_fusion
  238.2 1.8 fusion.37
  240.0 3.3 fusion.119
  244.9 4.2 fusion.120
  249.2 1.8 multiply_reduce_fusion
  252.5 2.3 pack.1
  256.6 2.7 convolution_convert_fusion.1
  259.4 2.2 copy-done.1
  261.5 1.4 convolution_convert_fusion
  263.8 1.5 copy-done
  265.2 9.3 %query_grad.1 = bf16[2,64,768]{2,1,0:T(8,128)(2,1)} custom-call(bf16[2,64,768]{2,1,0:T(8,128)(2,1)} %dynamic-slice_bitcast_fusion.2.q_ref, bf16[16,2,64,768]{3,2,1,0:T(8,128)(2,1)} %bitcast.438, bf16[16,2,64,768]{3,2,1,0:T(8,128)(2,1)} %bitcast.441, bf16[2,64,896]{2,1,0:T(8,128)(2,1)} %bitcast.457, s32[2,64,1]{2,1,0:T(8,128)} %copy.18.sq_ref.sk_ref, ...), custom_call_target="tpu_custom_call" | custom-call | flops 2415919104 | bytes 6291456 | tf_op jit(solution)/shard_map/query_grad/pallas_call | solution.py:212
  275.6 1.4 fusion.8
  277.1 4.6 fusion.117
  281.8 2.1 stack.110
  283.9 2.1 stack.111
  286.0 2.1 stack.112
  288.1 2.1 stack.113
  290.2 2.1 stack.114
  292.3 2.1 stack.115
  294.4 2.1 stack.116
  296.5 2.1 stack.117
  301.6 1.8 dynamic-slice_bitcast_fusion
  305.1 8.5 %key_grad.1 = (bf16[2,64,768]{2,1,0:T(8,128)(2,1)}, bf16[2,64,768]{2,1,0:T(8,128)(2,1)}) custom-call(bf16[2,64,768]{2,1,0:T(8,128)(2,1)} %get-tuple-element.106.k_ref, bf16[2,64,768]{2,1,0:T(8,128)(2,1)} %get-tuple-element.105.v_ref, bf16[16,2,64,768]{3,2,1,0:T(8,128)(2,1)} %bitcast.448, ...), custom_call_target="tpu_custom_call" | custom-call | flops 3221225472 | bytes 6291456 | tf_op jit(solution)/shard_map/key_grad/pallas_call | solution.py:238
  313.6 1.5 fusion.9
  316.5 1.4 fusion.10
  320.1 1.8 fusion.31
  321.9 1.9 fusion.28
  323.7 1.9 fusion.27
  325.6 1.8 fusion.32
  327.4 1.9 fusion.26
  332.6 1.9 constant_dynamic-update-slice_fusion.44
  353.0 1.8 convolution_add_fusion.2
  356.0 161.6 %reduce-scatter.2.cloned.1.call-done = bf16[1,304,768]{2,1,0:T(8,128)(2,1)} async-done(((bf16[32,304,768]{2,1,0:T(8,128)(2,1)}), bf16[1,304,768]{2,1,0:T(8,128)(2,1)}) %reduce-scatter.2.cloned.1.call-update) | async-done | bytes 466960 | tf_op jit(solution)/shard_map/reduce_scatter | solution.py:436
  (191 shorter events, 63.3 us)
Async XLA Ops:
  7.2 117.2 %all-gather.5.cloned.1.call-start = ((), (), s32[]{:S(2)}) async-start(), calls=%async_computation.1 | async-start | bytes 15409152 | tf_op jit(solution)/shard_map/all_gather | solution.py:343
  15.7 163.2 %all-gather.9.cloned.1.call-start = ((), (), s32[]{:S(2)}) async-start(), calls=%async_computation.4 | async-start | bytes 3342336 | tf_op jit(solution)/shard_map/all_gather | solution.py:342
  16.4 288.7 %all-gather.7.cloned.1.call-start = ((), (), s32[]{:S(2)}) async-start(), calls=%async_computation.2 | async-start | bytes 3899392 | tf_op jit(solution)/shard_map/all_gather | solution.py:399
  165.7 1.0 copy-start.26
  178.8 7.1 %copy-start.15 = (bf16[768,768]{1,0:T(8,128)(2,1)}, bf16[768,768]{1,0:T(8,128)(2,1)S(1)}, u32[]{:S(2)}) copy-start(bf16[768,768]{1,0:T(8,128)(2,1)S(1)} %get-tuple-element.85) | copy-start | bytes 3538948
  178.8 53.1 %copy-start.8 = (bf16[768,768]{1,0:T(8,128)(2,1)}, bf16[768,768]{1,0:T(8,128)(2,1)S(1)}, u32[]{:S(2)}) copy-start(bf16[768,768]{1,0:T(8,128)(2,1)S(1)} %get-tuple-element.86) | copy-start | bytes 3538948
  197.1 11.2 %copy-start.27 = (bf16[768,768]{1,0:T(8,128)(2,1)S(1)}, bf16[768,768]{1,0:T(8,128)(2,1)}, u32[]{:S(2)}) copy-start(bf16[768,768]{1,0:T(8,128)(2,1)} %copy-done.26) | copy-start | bytes 3538948
  210.2 6.6 %copy-start.28 = (bf16[768,768]{1,0:T(8,128)(2,1)}, bf16[768,768]{1,0:T(8,128)(2,1)S(1)}, u32[]{:S(2)}) copy-start(bf16[768,768]{1,0:T(8,128)(2,1)S(1)} %get-tuple-element.81) | copy-start | bytes 3538948
  221.5 10.5 %copy-start.7 = (bf16[2,1,64,768]{3,2,1,0:T(8,128)(2,1)S(1)}, bf16[2,1,64,768]{3,2,1,0:T(8,128)(2,1)}, u32[]{:S(2)}) copy-start(bf16[2,1,64,768]{3,2,1,0:T(8,128)(2,1)} %param.4) | copy-start | bytes 589828
  236.8 6.7 %copy-start.14 = (bf16[2,1,64,768]{3,2,1,0:T(8,128)(2,1)S(1)}, bf16[2,1,64,768]{3,2,1,0:T(8,128)(2,1)}, u32[]{:S(2)}) copy-start(bf16[2,1,64,768]{3,2,1,0:T(8,128)(2,1)} %param.7) | copy-start | bytes 589828
  244.6 4.6 slice-start
  244.9 6.1 %copy-start.10 = (f32[128,768]{1,0:T(8,128)}, f32[128,768]{1,0:T(8,128)S(1)}, u32[]{:S(2)}) copy-start(f32[128,768]{1,0:T(8,128)S(1)} %get-tuple-element.32) | copy-start | bytes 1179652
  244.9 4.3 slice-start.1
  249.1 3.4 copy-start.13
  249.1 2.1 copy-start.9
  251.0 4.0 copy-start.12
  254.9 262.8 %reduce-scatter.2.cloned.1.call-start = ((), (), s32[]{:S(2)}) async-start(), calls=%async_computation.3 | async-start | bytes 15409152 | tf_op jit(solution)/shard_map/reduce_scatter | solution.py:436
  255.5 1.1 copy-start.2
  256.6 4.9 copy-start.11
  259.3 2.2 copy-start.1
  263.0 2.3 copy-start
  277.0 27.3 %copy-start.6 = (bf16[768,768]{1,0:T(8,128)(2,1)}, bf16[768,768]{1,0:T(8,128)(2,1)S(1)}, u32[]{:S(2)}) copy-start(bf16[768,768]{1,0:T(8,128)(2,1)S(1)} %fusion.8) | copy-start | bytes 3538948
  281.8 19.0 %slice-start.5 = ((bf16[768,3072]{1,0:T(8,128)(2,1)}), bf16[24,3072]{1,0:T(8,128)(2,1)S(1)}, s32[]{:S(2)}) async-start(bf16[768,3072]{1,0:T(8,128)(2,1)} %copy-done.1), calls=%async_computation.10 | async-start | bytes 294912 | tf_op jit(solution)/shard_map/slice | solution.py:306
  313.6 6.4 %slice-start.8 = ((bf16[768,768]{1,0:T(8,128)(2,1)}), bf16[192,768]{1,0:T(8,128)(2,1)S(1)}, s32[]{:S(2)}) async-start(bf16[768,768]{1,0:T(8,128)(2,1)} %copy-done.6), calls=%async_computation.13 | async-start | bytes 589824 | tf_op jit(solution)/shard_map/slice | solution.py:306
  313.6 15.7 %copy-start.35 = (bf16[16,768]{1,0:T(8,128)(2,1)S(1)}, bf16[16,768]{1,0:T(8,128)(2,1)}, u32[]{:S(2)}) copy-start(bf16[16,768]{1,0:T(8,128)(2,1)} %slice.1130) | copy-start | bytes 73732
  315.1 1.4 copy-start.4
  315.1 15.0 %copy-start.3 = (bf16[768,768]{1,0:T(8,128)(2,1)S(1)}, bf16[768,768]{1,0:T(8,128)(2,1)}, u32[]{:S(2)}) copy-start(bf16[768,768]{1,0:T(8,128)(2,1)} %copy-done.2) | copy-start | bytes 3538948
  317.9 1.1 copy-start.5
  317.9 13.9 %slice-start.6 = ((bf16[768,768]{1,0:T(8,128)(2,1)}), bf16[192,768]{1,0:T(8,128)(2,1)S(1)}, s32[]{:S(2)}) async-start(bf16[768,768]{1,0:T(8,128)(2,1)} %copy-done.2), calls=%async_computation.11 | async-start | bytes 589824 | tf_op jit(solution)/shard_map/slice | solution.py:306
  319.0 10.3 %slice-start.7 = ((bf16[768,768]{1,0:T(8,128)(2,1)}), bf16[288,768]{1,0:T(8,128)(2,1)S(1)}, s32[]{:S(2)}) async-start(bf16[768,768]{1,0:T(8,128)(2,1)} %copy-done.5), calls=%async_computation.12 | async-start | bytes 884736 | tf_op jit(solution)/shard_map/slice | solution.py:306
  320.0 14.5 %copy-start.25 = (bf16[1,304,768]{2,1,0:T(8,128)(2,1)S(1)}, bf16[1,304,768]{2,1,0:T(8,128)(2,1)}, u32[]{:S(2)}) copy-start(bf16[1,304,768]{2,1,0:T(8,128)(2,1)} %stack.111) | copy-start | bytes 1400836
  321.8 13.5 %copy-start.24 = (bf16[1,304,768]{2,1,0:T(8,128)(2,1)S(1)}, bf16[1,304,768]{2,1,0:T(8,128)(2,1)}, u32[]{:S(2)}) copy-start(bf16[1,304,768]{2,1,0:T(8,128)(2,1)} %stack.112) | copy-start | bytes 1400836
  323.7 12.4 %copy-start.23 = (bf16[1,304,768]{2,1,0:T(8,128)(2,1)S(1)}, bf16[1,304,768]{2,1,0:T(8,128)(2,1)}, u32[]{:S(2)}) copy-start(bf16[1,304,768]{2,1,0:T(8,128)(2,1)} %stack.113) | copy-start | bytes 1400836
  325.6 11.3 %copy-start.22 = (bf16[1,304,768]{2,1,0:T(8,128)(2,1)S(1)}, bf16[1,304,768]{2,1,0:T(8,128)(2,1)}, u32[]{:S(2)}) copy-start(bf16[1,304,768]{2,1,0:T(8,128)(2,1)} %stack.114) | copy-start | bytes 1400836
  325.6 17.0 %slice-start.2 = ((s8[4718592]{0:T(1024)(128)(4,1)}), s8[524288]{0:T(1024)(128)(4,1)S(1)}, s32[]{:S(2)}) async-start(s8[4718592]{0:T(1024)(128)(4,1)} %bitcast.435), calls=%async_computation.7 | async-start | bytes 1048576
  327.4 10.3 %copy-start.21 = (bf16[1,304,768]{2,1,0:T(8,128)(2,1)S(1)}, bf16[1,304,768]{2,1,0:T(8,128)(2,1)}, u32[]{:S(2)}) copy-start(bf16[1,304,768]{2,1,0:T(8,128)(2,1)} %stack.115) | copy-start | bytes 1400836
  329.3 9.3 %copy-start.20 = (bf16[1,304,768]{2,1,0:T(8,128)(2,1)S(1)}, bf16[1,304,768]{2,1,0:T(8,128)(2,1)}, u32[]{:S(2)}) copy-start(bf16[1,304,768]{2,1,0:T(8,128)(2,1)} %stack.116) | copy-start | bytes 1400836
  330.1 9.3 %copy-start.19 = (bf16[1,304,768]{2,1,0:T(8,128)(2,1)S(1)}, bf16[1,304,768]{2,1,0:T(8,128)(2,1)}, u32[]{:S(2)}) copy-start(bf16[1,304,768]{2,1,0:T(8,128)(2,1)} %stack.117) | copy-start | bytes 1400836
  331.0 9.2 %copy-start.17 = (bf16[1,304,768]{2,1,0:T(8,128)(2,1)S(1)}, bf16[1,304,768]{2,1,0:T(8,128)(2,1)}, u32[]{:S(2)}) copy-start(bf16[1,304,768]{2,1,0:T(8,128)(2,1)} %stack.118) | copy-start | bytes 1400836
  331.8 9.2 %copy-start.18 = (bf16[1,304,768]{2,1,0:T(8,128)(2,1)S(1)}, bf16[1,304,768]{2,1,0:T(8,128)(2,1)}, u32[]{:S(2)}) copy-start(bf16[1,304,768]{2,1,0:T(8,128)(2,1)} %stack.119) | copy-start | bytes 1400836
  332.6 9.2 %copy-start.32 = (bf16[208,768]{1,0:T(8,128)(2,1)S(1)}, bf16[208,768]{1,0:T(8,128)(2,1)}, u32[]{:S(2)}) copy-start(bf16[208,768]{1,0:T(8,128)(2,1)} %slice.1146) | copy-start | bytes 958468
  332.6 9.2 %copy-start.34 = (bf16[96,768]{1,0:T(8,128)(2,1)S(1)}, bf16[96,768]{1,0:T(8,128)(2,1)}, u32[]{:S(2)}) copy-start(bf16[96,768]{1,0:T(8,128)(2,1)} %slice.1000) | copy-start | bytes 442372
  335.3 7.3 %slice-start.3 = ((s8[4718592]{0:T(1024)(128)(4,1)}), s8[4194304]{0:T(1024)(128)(4,1)S(1)}, s32[]{:S(2)}) async-start(s8[4718592]{0:T(1024)(128)(4,1)} %bitcast.435), calls=%async_computation.8 | async-start | bytes 8388608
  341.9 8.1 %slice-start.4 = ((bf16[3072,768]{1,0:T(8,128)(2,1)}), bf16[288,768]{1,0:T(8,128)(2,1)S(1)}, s32[]{:S(2)}) async-start(bf16[3072,768]{1,0:T(8,128)(2,1)} %copy-done), calls=%async_computation.9 | async-start | bytes 884736 | tf_op jit(solution)/shard_map/slice | solution.py:306
  351.1 1.3 copy-start.16
  351.1 1.3 copy-start.30
  351.1 1.8 copy-start.33
  351.1 3.6 copy-start.29
  351.2 3.6 copy-start.31
Sparse Core Ops, SparseCore 0:
  15.8 108.5 all-gather.4
  126.7 43.7 all-gather.8
  255.0 46.0 all-gather.6
  351.3 166.2 reduce-scatter.1
